TPU v7x, 128 devices: a whole 4x4x4 slice. The times are simulated.
128 devices in a mesh: rep: 16 (over y, z), tp: 8 (over x, core).
Axes of the slice: x: 4, y: 4, z: 4, core: 2. Of those that a mesh axis runs over, the one named last changes fastest.
Arguments:
- grads: bfloat16 [16, 12, 768, 2048], P('rep', None, None, 'tp'), may hold values from -6 to 6
- error: float32 [16, 12, 768, 2048], P('rep', None, None, 'tp'), may hold values from -2 to 2
- query: float32 [12, 32, 2048], P(None, None, 'tp'), may hold values from -6 to 6
- momentum: float32 [9216, 2048], P(('rep', 'tp')), may hold values from -0.8 to 0.8
- master: float32 [9216, 2048], P(('rep', 'tp')), may hold values from -0.8 to 0.8
Outputs:
- new_error: float32 [16, 12, 768, 2048], P('rep', None, None, 'tp')
- new_query: float32 [12, 32, 2048], P(None, None, 'tp')
- new_momentum: float32 [9216, 2048], P(('rep', 'tp'))
- new_master: float32 [9216, 2048], P(('rep', 'tp'))
- weights: bfloat16 [12, 768, 2048], P(None, None, 'tp')
All inputs are finite; a program needn't handle non-finite values.
Results may differ from a plain program's by a relative error of at most 0.0004.
Values may be sent and summed in bfloat16 or wider, within the bound.
A program may use at most 128 MiB of HBM per device.

v0:
```python
import jax
import jax.numpy as jnp
from jax import lax
from jax.sharding import PartitionSpec as P

ROUNDS = 2
NS_STEPS = 5
NORM_EPSILON = 1e-06
MOMENTUM_DECAY = 0.9
LEARNING_RATE = 0.5


def local_gram(factor):
    return jnp.einsum("krd,ksd->krs", factor, factor, precision=lax.Precision.HIGHEST)


def orthonormal(factor, gram_of):
    gram_now = gram_of(factor)
    sum_squares = jnp.trace(gram_now, axis1=1, axis2=2)[:, None, None]
    factor_scale = lax.rsqrt(sum_squares + NORM_EPSILON)
    ortho_basis = factor * factor_scale
    gram_now = gram_now * (factor_scale * factor_scale)
    for iteration in range(NS_STEPS):
        if iteration > 0:
            gram_now = gram_of(ortho_basis)
        ortho_basis = 1.5 * ortho_basis - 0.5 * jnp.einsum(
            "krs,ksd->krd", gram_now, ortho_basis, precision=lax.Precision.HIGHEST
        )
    return ortho_basis


def local(grads, error, query, momentum, master):
    corrected = grads[0].astype(jnp.float32) + error[0]
    current = query
    replicas = lax.axis_size("rep")
    for power_pass in range(ROUNDS):
        partial_factor = jnp.einsum(
            "kdf,krf->krd", corrected, current, precision=lax.Precision.HIGHEST
        )
        summed = lax.psum(partial_factor, ("rep", "tp"))
        ortho_basis = orthonormal(summed, local_gram)
        partial_query = jnp.einsum(
            "kdf,krd->krf", corrected, ortho_basis, precision=lax.Precision.HIGHEST
        )
        current = lax.psum(partial_query, "rep") / replicas
    approx = jnp.einsum("krd,krf->kdf", ortho_basis, current, precision=lax.Precision.HIGHEST)
    new_error = (corrected - approx)[None]
    matrices, model_width, shard_cols = approx.shape
    block_rows = matrices * model_width // replicas
    approx_rows = approx.reshape(matrices * model_width, shard_cols)
    own_block = lax.dynamic_slice_in_dim(
        approx_rows, lax.axis_index("rep") * block_rows, block_rows, 0
    )
    flat_approx = lax.all_to_all(own_block, "tp", split_axis=0, concat_axis=1, tiled=True)
    new_momentum = MOMENTUM_DECAY * momentum + flat_approx
    new_master = master - LEARNING_RATE * new_momentum
    working = new_master.astype(jnp.bfloat16)
    by_columns = lax.all_to_all(working, "tp", split_axis=1, concat_axis=0, tiled=True)
    weight_rows = lax.all_gather(by_columns, "rep", axis=0, tiled=True)
    weights = weight_rows.reshape(matrices, model_width, shard_cols)
    return (new_error, current, new_momentum, new_master, weights)


def solution(mesh):
    placed = (
        P("rep", None, None, "tp"),
        P("rep", None, None, "tp"),
        P(None, None, "tp"),
        P(("rep", "tp"), None),
        P(("rep", "tp"), None),
    )
    return jax.shard_map(
        local,
        mesh=mesh,
        in_specs=placed,
        out_specs=(
            P("rep", None, None, "tp"),
            P(None, None, "tp"),
            P(("rep", "tp"), None),
            P(("rep", "tp"), None),
            P(None, None, "tp"),
        ),
        check_vma=False,
    )
```

profile of v0, /device:TPU:1, one launch (start us, length us, event | category | flops | bytes accessed | tf_op | source)
XLA Modules:
  0.0 643.5 jit_solution(3805032442626660912)
XLA Ops:
  8.2 14.9 %fusion.9 = f32[12,32,768]{2,1,0:T(8,128)} fusion(f32[12,32,256]{2,1,0:T(8,128)S(1)} %copy-done, f32[1,12,768,256]{3,2,1,0:T(8,128)} %param.6, bf16[1,12,768,256]{3,2,1,0:T(8,128)(2,1)} %param.5), kind=kOutput, calls=%fused_computation.11 | convolution fusion | flops 910688256 | bytes 15728640 | tf_op jit(solution)/shard_map/kdf,krf->krd/dot_general | solution.py:37
  23.3 150.7 %all-reduce.5.cloned.1.call-done = f32[12,32,768]{2,1,0:T(8,128)} async-done(((f32[12,32,768]{2,1,0:T(8,128)}), f32[12,32,768]{2,1,0:T(8,128)}) %all-reduce.5.cloned.1.call-update) | async-done | bytes 1179664 | tf_op jit(solution)/shard_map/psum | solution.py:40
  174.1 3.0 select_reduce_fusion.1
  177.1 1.3 fusion.21
  179.6 1.2 fusion.20
  180.9 1.2 fusion.37
  183.3 1.2 fusion.38
  185.7 1.2 fusion.39
  188.6 6.7 %fusion.4 = f32[12,32,256]{2,1,0:T(8,128)} fusion(f32[12,32,768]{2,1,0:T(8,128)S(1)} %fusion.17, f32[1,12,768,256]{3,2,1,0:T(8,128)S(1)} %bitcast.73, bf16[1,12,768,256]{3,2,1,0:T(8,128)(2,1)S(1)} %bitcast.77), kind=kOutput, calls=%fused_computation.5 | convolution fusion | flops 910688256 | bytes 15728640 | tf_op jit(solution)/shard_map/kdf,krd->krf/dot_general | solution.py:42
  195.4 81.4 %all-reduce.7.cloned.1.call-done = f32[12,32,256]{2,1,0:T(8,128)} async-done(((f32[12,32,256]{2,1,0:T(8,128)}), f32[12,32,256]{2,1,0:T(8,128)}) %all-reduce.7.cloned.1.call-update) | async-done | bytes 393232 | tf_op jit(solution)/shard_map/psum | solution.py:45
  276.8 14.6 %fusion.2 = f32[12,32,768]{2,1,0:T(8,128)} fusion(f32[12,32,256]{2,1,0:T(8,128)} %all-reduce.7.cloned.1.call-done, f32[1,12,768,256]{3,2,1,0:T(8,128)} %param.6, bf16[1,12,768,256]{3,2,1,0:T(8,128)(2,1)} %param.5), kind=kOutput, calls=%fused_computation.3 | convolution fusion | flops 910786560 | bytes 15728640 | tf_op jit(solution)/shard_map/kdf,krf->krd/dot_general | solution.py:37
  291.6 148.1 %all-reduce.9.cloned.1.call-done = f32[12,32,768]{2,1,0:T(8,128)} async-done(((f32[12,32,768]{2,1,0:T(8,128)}), f32[12,32,768]{2,1,0:T(8,128)}) %all-reduce.9.cloned.1.call-update) | async-done | bytes 1179664 | tf_op jit(solution)/shard_map/psum | solution.py:40
  439.7 3.0 select_reduce_fusion
  442.7 1.3 fusion.16
  444.0 1.2 fusion.40
  445.3 1.2 fusion.15
  454.0 6.8 %fusion = f32[12,32,256]{2,1,0:T(8,128)} fusion(f32[12,32,768]{2,1,0:T(8,128)S(1)} %fusion.12, f32[1,12,768,256]{3,2,1,0:T(8,128)S(1)} %bitcast.75, bf16[1,12,768,256]{3,2,1,0:T(8,128)(2,1)S(1)} %bitcast.79), kind=kOutput, calls=%fused_computation.1 | convolution fusion | flops 910688256 | bytes 15728640 | tf_op jit(solution)/shard_map/kdf,krd->krf/dot_general | solution.py:42
  460.8 81.4 %all-reduce.11.cloned.1.call-done = f32[12,32,256]{2,1,0:T(8,128)} async-done(((f32[12,32,256]{2,1,0:T(8,128)}), f32[12,32,256]{2,1,0:T(8,128)}) %all-reduce.11.cloned.1.call-update) | async-done | bytes 393232 | tf_op jit(solution)/shard_map/psum | solution.py:45
  543.3 7.7 %fusion.44 = f32[12,768,256]{2,1,0:T(8,128)S(1)} fusion(f32[12,32,768]{2,1,0:T(8,128)S(1)} %fusion.12, f32[12,32,256]{2,1,0:T(8,128)S(1)} %broadcast_multiply_fusion), kind=kOutput, calls=%fused_computation.64 | convolution fusion | flops 905969664 | bytes 11010048 | tf_op jit(solution)/shard_map/krd,krf->kdf/dot_general | solution.py:46
  551.1 16.7 %all_to_all.38 = f32[8,72,256]{2,1,0:T(8,128)S(1)} all-to-all(f32[8,72,256]{2,1,0:T(8,128)S(1)} %bitcast.83), channel_id=1, replica_groups=mesh['rep'=16,'tp'=8] {'tp'}, dimensions={0} | all-to-all | bytes 1179648 | tf_op jit(solution)/shard_map/all_to_all | solution.py:54
  569.1 11.1 %all_to_all.39 = bf16[72,8,256]{2,0,1:T(8,128)(2,1)} all-to-all(bf16[72,8,256]{2,0,1:T(8,128)(2,1)S(1)} %bitcast.87), channel_id=1, replica_groups=mesh['rep'=16,'tp'=8] {'tp'}, dimensions={1} | all-to-all | bytes 589824 | tf_op jit(solution)/shard_map/all_to_all | solution.py:58
  580.3 12.7 %fusion.8 = f32[1,12,768,256]{3,2,1,0:T(8,128)} fusion(f32[12,768,256]{2,1,0:T(8,128)} %copy-done.2, f32[1,12,768,256]{3,2,1,0:T(8,128)} %param.6, bf16[1,12,768,256]{3,2,1,0:T(8,128)(2,1)} %param.5), kind=kLoop, calls=%fused_computation.9 | loop fusion | flops 7077888 | bytes 33030144 | tf_op jit(solution)/shard_map/broadcast_in_dim | solution.py:47
  592.9 38.9 %all-gather.2.cloned.1.call-done = bf16[9216,256]{1,0:T(8,128)(2,1)} async-done(((bf16[576,256]{1,0:T(8,128)(2,1)}), bf16[9216,256]{1,0:T(8,128)(2,1)}) %all-gather.2.cloned.1.call-update) | async-done | bytes 4718608 | tf_op jit(solution)/shard_map/all_gather | solution.py:59
  631.8 4.9 copy.24
  (68 shorter events, 16.4 us)
Async XLA Ops:
  7.2 1.0 copy-start
  7.2 166.9 %all-reduce.5.cloned.1.call-start = ((), (), s32[]{:S(2)}) async-start(), calls=%async_computation.2 | async-start | bytes 2359296 | tf_op jit(solution)/shard_map/psum | solution.py:40
  23.1 253.7 %all-reduce.7.cloned.1.call-start = ((), (), s32[]{:S(2)}) async-start(), calls=%async_computation.3 | async-start | bytes 786432 | tf_op jit(solution)/shard_map/psum | solution.py:45
  174.1 3.0 copy-start.3
  178.4 9.7 %slice-start = ((s8[9437184]{0:T(1024)(128)(4,1)}), s8[4194304]{0:T(1024)(128)(4,1)S(1)}, s32[]{:S(2)}) async-start(s8[9437184]{0:T(1024)(128)(4,1)} %bitcast.72), calls=%async_computation.7 | async-start | bytes 8388608
  179.6 8.9 %slice-start.6 = ((s8[4718592]{0:T(1024)(128)(4,1)}), s8[4194304]{0:T(1024)(128)(4,1)S(1)}, s32[]{:S(2)}) async-start(s8[4718592]{0:T(1024)(128)(4,1)} %bitcast.76), calls=%async_computation.13 | async-start | bytes 8388608
  180.9 7.6 %slice-start.1 = ((s8[9437184]{0:T(1024)(128)(4,1)}), s8[4194304]{0:T(1024)(128)(4,1)S(1)}, s32[]{:S(2)}) async-start(s8[9437184]{0:T(1024)(128)(4,1)} %bitcast.72), calls=%async_computation.8 | async-start | bytes 8388608
  183.3 5.3 slice-start.7
  184.5 4.0 slice-start.2
  195.3 244.4 %all-reduce.9.cloned.1.call-start = ((), (), s32[]{:S(2)}) async-start(), calls=%async_computation.4 | async-start | bytes 2359296 | tf_op jit(solution)/shard_map/psum | solution.py:40
  291.4 250.9 %all-reduce.11.cloned.1.call-start = ((), (), s32[]{:S(2)}) async-start(), calls=%async_computation.5 | async-start | bytes 786432 | tf_op jit(solution)/shard_map/psum | solution.py:45
  439.7 3.0 copy-start.4
  444.0 9.7 %slice-start.3 = ((s8[9437184]{0:T(1024)(128)(4,1)}), s8[4194304]{0:T(1024)(128)(4,1)S(1)}, s32[]{:S(2)}) async-start(s8[9437184]{0:T(1024)(128)(4,1)} %bitcast.74), calls=%async_computation.10 | async-start | bytes 8388608
  445.2 8.5 %slice-start.8 = ((s8[4718592]{0:T(1024)(128)(4,1)}), s8[4194304]{0:T(1024)(128)(4,1)S(1)}, s32[]{:S(2)}) async-start(s8[4718592]{0:T(1024)(128)(4,1)} %bitcast.78), calls=%async_computation.15 | async-start | bytes 8388608
  446.5 7.2 %slice-start.4 = ((s8[9437184]{0:T(1024)(128)(4,1)}), s8[4194304]{0:T(1024)(128)(4,1)S(1)}, s32[]{:S(2)}) async-start(s8[9437184]{0:T(1024)(128)(4,1)} %bitcast.74), calls=%async_computation.11 | async-start | bytes 8388608
  448.9 4.8 slice-start.9
  450.1 3.8 slice-start.5
  460.8 171.1 %all-gather.2.cloned.1.call-start = ((), (), s32[]{:S(2)}) async-start(), calls=%async_computation.6 | async-start | bytes 5013504 | tf_op jit(solution)/shard_map/all_gather | solution.py:59
  543.3 7.8 %copy-start.5 = (f32[12,32,256]{2,1,0:T(8,128)}, f32[12,32,256]{2,1,0:T(8,128)S(1)}, u32[]{:S(2)}) copy-start(f32[12,32,256]{2,1,0:T(8,128)S(1)} %broadcast_multiply_fusion) | copy-start | bytes 1179652
  551.0 18.1 %copy-start.2 = (f32[12,768,256]{2,1,0:T(8,128)}, f32[12,768,256]{2,1,0:T(8,128)S(1)}, u32[]{:S(2)}) copy-start(f32[12,768,256]{2,1,0:T(8,128)S(1)} %fusion.44) | copy-start | bytes 28311556
  551.1 16.8 %copy-start.6 = (f32[72,2048]{1,0:T(8,128)S(1)}, f32[72,2048]{1,0:T(8,128)}, u32[]{:S(2)}) copy-start(f32[72,2048]{1,0:T(8,128)} %param.9) | copy-start | bytes 1769476
  551.1 16.8 %copy-start.7 = (f32[72,2048]{1,0:T(8,128)S(1)}, f32[72,2048]{1,0:T(8,128)}, u32[]{:S(2)}) copy-start(f32[72,2048]{1,0:T(8,128)} %param.8) | copy-start | bytes 1769476
  631.8 4.9 copy-start.1
Sparse Core Ops, SparseCore 0:
  23.2 150.8 all-reduce.4
  195.4 81.3 all-reduce.6
  291.5 148.1 all-reduce.8
  460.9 81.3 all-reduce.10
  580.4 51.3 all-gather.1
where the time goes:
time: 649 us; the launch traced here: 643 us
  waiting for transfers between devices  501 us (77%)
  matrix products  78.5 us (12%)
  blocking collectives  27.8 us (4%)
  other arithmetic  14.9 us (2%)
  between operations  14.6 us (2%)
    psum x2, waiting for transfers between devices, local(): summed = lax.psum(partial_factor, ('rep', 'tp'))  299 us
    psum x2, waiting for transfers between devices, local(): current = lax.psum(partial_query, 'rep') / replicas  163 us
    all_gather x1, waiting for transfers between devices, local(): weight_rows = lax.all_gather(by_columns, 'rep', axis=0, tiled=True)  38.9 us
    dot_general x2, matrix products, local(): jnp.einsum('kdf,krf->krd', corrected, current, precision=lax.Precision.HI...  29.5 us
    all_to_all x1, blocking collectives, local(): lax.all_to_all(own_block, 'tp', split_axis=0, concat_axis=1, tiled=True)  16.7 us
    dot_general x10, matrix products, local_gram(): jnp.einsum('krd,ksd->krs', factor, factor, precision=lax.Precision.HIGHEST)  15.7 us
    dot_general x2, matrix products, local(): jnp.einsum('kdf,krd->krf', corrected, ortho_basis, precision=lax.Precisio...  13.5 us
  transfers between devices with their start and end apart: 5, of which 5 were waited for; matrix products, arithmetic and copies ran while one was open for 2% of the time, Pallas kernels for 0%

commit v1 on v0

--- a/solution.py
+++ b/solution.py
@@ -51,7 +51,9 @@
     own_block = lax.dynamic_slice_in_dim(
         approx_rows, lax.axis_index("rep") * block_rows, block_rows, 0
     )
-    flat_approx = lax.all_to_all(own_block, "tp", split_axis=0, concat_axis=1, tiled=True)
+    shards = jnp.split(own_block, lax.axis_size("tp"), axis=0)
+    received = lax.all_to_all(jnp.stack(shards), "tp", 0, 0)
+    flat_approx = jnp.concatenate(received, axis=1)
     new_momentum = MOMENTUM_DECAY * momentum + flat_approx
     new_master = master - LEARNING_RATE * new_momentum
     working = new_master.astype(jnp.bfloat16)

time: 649 us -> 650 us (level)
  no operation moved by 1% of the time
where the time goes in v1:
time: 650 us; the launch traced here: 644 us
  waiting for transfers between devices  501 us (77%)
  matrix products  78.5 us (12%)
  blocking collectives  27.8 us (4%)
  other arithmetic  14.9 us (2%)
  between operations  14.7 us (2%)
  local copies, waits for them, and re-layouts  6.54 us (1%)
    psum x2, waiting for transfers between devices, local(): summed = lax.psum(partial_factor, ('rep', 'tp'))  299 us
    psum x2, waiting for transfers between devices, local(): current = lax.psum(partial_query, 'rep') / replicas  163 us
    all_gather x1, waiting for transfers between devices, local(): weight_rows = lax.all_gather(by_columns, 'rep', axis=0, tiled=True)  38.9 us
    dot_general x2, matrix products, local(): jnp.einsum('kdf,krf->krd', corrected, current, precision=lax.Precision.HI...  29.5 us
    all_to_all x1, blocking collectives, local(): received = lax.all_to_all(jnp.stack(shards), 'tp', 0, 0)  16.7 us
    dot_general x10, matrix products, local_gram(): jnp.einsum('krd,ksd->krs', factor, factor, precision=lax.Precision.HIGHEST)  15.7 us
    dot_general x2, matrix products, local(): jnp.einsum('kdf,krd->krf', corrected, ortho_basis, precision=lax.Precisio...  13.5 us
  transfers between devices with their start and end apart: 5, of which 5 were waited for; matrix products, arithmetic and copies ran while one was open for 2% of the time, Pallas kernels for 0%

profile of v1, /device:TPU:1, one launch (start us, length us, event | category | flops | bytes accessed | tf_op | source)
XLA Modules:
  0.0 643.6 jit_solution(8427601370717528283)
XLA Ops:
  8.2 14.9 %fusion.9 = f32[12,32,768]{2,1,0:T(8,128)} fusion(f32[12,32,256]{2,1,0:T(8,128)S(1)} %copy-done, f32[1,12,768,256]{3,2,1,0:T(8,128)} %param.6, bf16[1,12,768,256]{3,2,1,0:T(8,128)(2,1)} %param.5), kind=kOutput, calls=%fused_computation.11 | convolution fusion | flops 910688256 | bytes 15728640 | tf_op jit(solution)/shard_map/kdf,krf->krd/dot_general | solution.py:37
  23.3 150.7 %all-reduce.5.cloned.1.call-done = f32[12,32,768]{2,1,0:T(8,128)} async-done(((f32[12,32,768]{2,1,0:T(8,128)}), f32[12,32,768]{2,1,0:T(8,128)}) %all-reduce.5.cloned.1.call-update) | async-done | bytes 1179664 | tf_op jit(solution)/shard_map/psum | solution.py:40
  174.1 3.0 select_reduce_fusion.1
  177.1 1.3 fusion.21
  179.6 1.2 fusion.20
  180.9 1.2 fusion.45
  183.3 1.2 fusion.46
  185.7 1.2 fusion.47
  188.6 6.7 %fusion.4 = f32[12,32,256]{2,1,0:T(8,128)} fusion(f32[12,32,768]{2,1,0:T(8,128)S(1)} %fusion.17, f32[1,12,768,256]{3,2,1,0:T(8,128)S(1)} %bitcast.104, bf16[1,12,768,256]{3,2,1,0:T(8,128)(2,1)S(1)} %bitcast.108), kind=kOutput, calls=%fused_computation.5 | convolution fusion | flops 910688256 | bytes 15728640 | tf_op jit(solution)/shard_map/kdf,krd->krf/dot_general | solution.py:42
  195.4 81.4 %all-reduce.7.cloned.1.call-done = f32[12,32,256]{2,1,0:T(8,128)} async-done(((f32[12,32,256]{2,1,0:T(8,128)}), f32[12,32,256]{2,1,0:T(8,128)}) %all-reduce.7.cloned.1.call-update) | async-done | bytes 393232 | tf_op jit(solution)/shard_map/psum | solution.py:45
  276.8 14.6 %fusion.2 = f32[12,32,768]{2,1,0:T(8,128)} fusion(f32[12,32,256]{2,1,0:T(8,128)} %all-reduce.7.cloned.1.call-done, f32[1,12,768,256]{3,2,1,0:T(8,128)} %param.6, bf16[1,12,768,256]{3,2,1,0:T(8,128)(2,1)} %param.5), kind=kOutput, calls=%fused_computation.3 | convolution fusion | flops 910786560 | bytes 15728640 | tf_op jit(solution)/shard_map/kdf,krf->krd/dot_general | solution.py:37
  291.6 148.1 %all-reduce.9.cloned.1.call-done = f32[12,32,768]{2,1,0:T(8,128)} async-done(((f32[12,32,768]{2,1,0:T(8,128)}), f32[12,32,768]{2,1,0:T(8,128)}) %all-reduce.9.cloned.1.call-update) | async-done | bytes 1179664 | tf_op jit(solution)/shard_map/psum | solution.py:40
  439.7 3.0 select_reduce_fusion
  442.7 1.3 fusion.16
  444.0 1.2 fusion.48
  445.3 1.2 fusion.15
  454.0 6.8 %fusion = f32[12,32,256]{2,1,0:T(8,128)} fusion(f32[12,32,768]{2,1,0:T(8,128)S(1)} %fusion.12, f32[1,12,768,256]{3,2,1,0:T(8,128)S(1)} %bitcast.106, bf16[1,12,768,256]{3,2,1,0:T(8,128)(2,1)S(1)} %bitcast.110), kind=kOutput, calls=%fused_computation.1 | convolution fusion | flops 910688256 | bytes 15728640 | tf_op jit(solution)/shard_map/kdf,krd->krf/dot_general | solution.py:42
  460.8 81.4 %all-reduce.11.cloned.1.call-done = f32[12,32,256]{2,1,0:T(8,128)} async-done(((f32[12,32,256]{2,1,0:T(8,128)}), f32[12,32,256]{2,1,0:T(8,128)}) %all-reduce.11.cloned.1.call-update) | async-done | bytes 393232 | tf_op jit(solution)/shard_map/psum | solution.py:45
  543.3 7.7 %fusion.52 = f32[12,768,256]{2,1,0:T(8,128)S(1)} fusion(f32[12,32,768]{2,1,0:T(8,128)S(1)} %fusion.12, f32[12,32,256]{2,1,0:T(8,128)S(1)} %broadcast_multiply_fusion), kind=kOutput, calls=%fused_computation.79 | convolution fusion | flops 905969664 | bytes 11010048 | tf_op jit(solution)/shard_map/krd,krf->kdf/dot_general | solution.py:46
  551.3 16.7 %all_to_all.24 = f32[8,72,256]{2,1,0:T(8,128)S(1)} all-to-all(f32[8,72,256]{2,1,0:T(8,128)S(1)} %fusion.32), channel_id=1, replica_groups=mesh['rep'=16,'tp'=8] {'tp'}, dimensions={0} | all-to-all | bytes 1179648 | tf_op jit(solution)/shard_map/all_to_all | solution.py:55
  569.2 11.1 %all_to_all.25 = bf16[72,8,256]{2,0,1:T(8,128)(2,1)} all-to-all(bf16[72,8,256]{2,0,1:T(8,128)(2,1)S(1)} %bitcast.124), channel_id=1, replica_groups=mesh['rep'=16,'tp'=8] {'tp'}, dimensions={1} | all-to-all | bytes 589824 | tf_op jit(solution)/shard_map/all_to_all | solution.py:60
  580.4 12.7 %fusion.8 = f32[1,12,768,256]{3,2,1,0:T(8,128)} fusion(f32[12,768,256]{2,1,0:T(8,128)} %copy-done.2, f32[1,12,768,256]{3,2,1,0:T(8,128)} %param.6, bf16[1,12,768,256]{3,2,1,0:T(8,128)(2,1)} %param.5), kind=kLoop, calls=%fused_computation.9 | loop fusion | flops 7077888 | bytes 33030144 | tf_op jit(solution)/shard_map/broadcast_in_dim | solution.py:47
  593.1 38.9 %all-gather.2.cloned.1.call-done = bf16[9216,256]{1,0:T(8,128)(2,1)} async-done(((bf16[576,256]{1,0:T(8,128)(2,1)}), bf16[9216,256]{1,0:T(8,128)(2,1)}) %all-gather.2.cloned.1.call-update) | async-done | bytes 4718608 | tf_op jit(solution)/shard_map/all_gather | solution.py:61
  632.0 4.9 copy.31
  (75 shorter events, 16.4 us)
Async XLA Ops:
  7.2 1.0 copy-start
  7.2 166.9 %all-reduce.5.cloned.1.call-start = ((), (), s32[]{:S(2)}) async-start(), calls=%async_computation.2 | async-start | bytes 2359296 | tf_op jit(solution)/shard_map/psum | solution.py:40
  23.1 253.7 %all-reduce.7.cloned.1.call-start = ((), (), s32[]{:S(2)}) async-start(), calls=%async_computation.3 | async-start | bytes 786432 | tf_op jit(solution)/shard_map/psum | solution.py:45
  174.1 3.0 copy-start.3
  178.4 9.7 %slice-start = ((s8[9437184]{0:T(1024)(128)(4,1)}), s8[4194304]{0:T(1024)(128)(4,1)S(1)}, s32[]{:S(2)}) async-start(s8[9437184]{0:T(1024)(128)(4,1)} %bitcast.103), calls=%async_computation.7 | async-start | bytes 8388608
  179.6 8.9 %slice-start.6 = ((s8[4718592]{0:T(1024)(128)(4,1)}), s8[4194304]{0:T(1024)(128)(4,1)S(1)}, s32[]{:S(2)}) async-start(s8[4718592]{0:T(1024)(128)(4,1)} %bitcast.107), calls=%async_computation.13 | async-start | bytes 8388608
  180.9 7.6 %slice-start.1 = ((s8[9437184]{0:T(1024)(128)(4,1)}), s8[4194304]{0:T(1024)(128)(4,1)S(1)}, s32[]{:S(2)}) async-start(s8[9437184]{0:T(1024)(128)(4,1)} %bitcast.103), calls=%async_computation.8 | async-start | bytes 8388608
  183.3 5.3 slice-start.7
  184.5 4.0 slice-start.2
  195.3 244.4 %all-reduce.9.cloned.1.call-start = ((), (), s32[]{:S(2)}) async-start(), calls=%async_computation.4 | async-start | bytes 2359296 | tf_op jit(solution)/shard_map/psum | solution.py:40
  291.4 250.9 %all-reduce.11.cloned.1.call-start = ((), (), s32[]{:S(2)}) async-start(), calls=%async_computation.5 | async-start | bytes 786432 | tf_op jit(solution)/shard_map/psum | solution.py:45
  439.7 3.0 copy-start.4
  444.0 9.7 %slice-start.3 = ((s8[9437184]{0:T(1024)(128)(4,1)}), s8[4194304]{0:T(1024)(128)(4,1)S(1)}, s32[]{:S(2)}) async-start(s8[9437184]{0:T(1024)(128)(4,1)} %bitcast.105), calls=%async_computation.10 | async-start | bytes 8388608
  445.2 8.5 %slice-start.8 = ((s8[4718592]{0:T(1024)(128)(4,1)}), s8[4194304]{0:T(1024)(128)(4,1)S(1)}, s32[]{:S(2)}) async-start(s8[4718592]{0:T(1024)(128)(4,1)} %bitcast.109), calls=%async_computation.15 | async-start | bytes 8388608
  446.5 7.2 %slice-start.4 = ((s8[9437184]{0:T(1024)(128)(4,1)}), s8[4194304]{0:T(1024)(128)(4,1)S(1)}, s32[]{:S(2)}) async-start(s8[9437184]{0:T(1024)(128)(4,1)} %bitcast.105), calls=%async_computation.11 | async-start | bytes 8388608
  448.9 4.8 slice-start.9
  450.1 3.8 slice-start.5
  460.8 171.2 %all-gather.2.cloned.1.call-start = ((), (), s32[]{:S(2)}) async-start(), calls=%async_computation.6 | async-start | bytes 5013504 | tf_op jit(solution)/shard_map/all_gather | solution.py:61
  543.3 7.8 %copy-start.5 = (f32[12,32,256]{2,1,0:T(8,128)}, f32[12,32,256]{2,1,0:T(8,128)S(1)}, u32[]{:S(2)}) copy-start(f32[12,32,256]{2,1,0:T(8,128)S(1)} %broadcast_multiply_fusion) | copy-start | bytes 1179652
  551.0 18.2 %copy-start.2 = (f32[12,768,256]{2,1,0:T(8,128)}, f32[12,768,256]{2,1,0:T(8,128)S(1)}, u32[]{:S(2)}) copy-start(f32[12,768,256]{2,1,0:T(8,128)S(1)} %fusion.52) | copy-start | bytes 28311556
  551.2 16.8 %copy-start.6 = (f32[72,2048]{1,0:T(8,128)S(1)}, f32[72,2048]{1,0:T(8,128)}, u32[]{:S(2)}) copy-start(f32[72,2048]{1,0:T(8,128)} %param.9) | copy-start | bytes 1769476
  551.3 16.8 %copy-start.7 = (f32[72,2048]{1,0:T(8,128)S(1)}, f32[72,2048]{1,0:T(8,128)}, u32[]{:S(2)}) copy-start(f32[72,2048]{1,0:T(8,128)} %param.8) | copy-start | bytes 1769476
  632.0 4.9 copy-start.1
Sparse Core Ops, SparseCore 0:
  23.2 150.8 all-reduce.4
  195.4 81.3 all-reduce.6
  291.5 148.1 all-reduce.8
  460.9 81.3 all-reduce.10
  580.5 51.3 all-gather.1
